TPU v7x, 32 devices: a whole 2x2x4 slice. The times are simulated.
32 devices in a mesh: windows: 2 (over x), tiles: 16 (over z, y, core).
Axes of the slice: x: 2, y: 2, z: 4, core: 2. Of those that a mesh axis runs over, the one named last changes fastest.
Arguments:
- data: bfloat16 [16, 2, 2048, 128], P('windows', None, 'tiles'), parts along dimension 0, may hold values from -6 to 6
- wavelet: float32 [8, 2], replicated, may hold values from -4 to 4
- panel_block: int32 [1], replicated, may hold values from 0 to 15
- tiles: bfloat16 [512, 2, 128, 128], P(('windows', 'tiles')), parts along dimension 0, may hold values from -0.25 to 0.25
- cover_rows: int32 [512], P(('windows', 'tiles')), parts along dimension 0, may hold values from 0 to 15, as said below
- cover_freqs: int32 [512], P(('windows', 'tiles')), parts along dimension 0, may hold values from 0 to 7
Outputs:
- residual: float32 [16, 2, 2048, 128], P('windows', None, 'tiles'), parts along dimension 0
- gradient: bfloat16 [512, 2, 128, 128], P(('windows', 'tiles')), parts along dimension 0
There are 2 independent parts, one for each index of `windows`. A program takes and returns all parts, laid end to end along the dimension named above; an argument that names none is the same for every part. Nothing has to cross between parts.
Inputs may be any that keep to these rules, and one draw needn't show every extreme that they name: `cover_rows`: among the 16 entries of one column block no row block appears more than 2 times, exactly 12 distinct row blocks appear, one row block appears 2 times in every column block, and together with cover_freqs the entries of one column block name distinct (row block, frequency) pairs.
All inputs are finite; a program needn't handle non-finite values.
Results may differ from a plain program's by a relative error of at most 0.0053.
Values may be sent and summed in bfloat16 or wider, within the bound.
A program may use at most 128 MiB of HBM per device.

v0:
```python
import jax
import jax.numpy as jnp
from jax import lax
from jax.sharding import PartitionSpec as P

CAP = 2


def complex_product(left, right):
    real_in = left[:, 0]
    imag_in = left[:, 1]
    stacked = jnp.stack(
        [jnp.stack([real_in, -imag_in], axis=1), jnp.stack([imag_in, real_in], axis=1)], axis=1
    )
    return jnp.einsum("sxyab,sybp->sxap", stacked, right, preferred_element_type=jnp.float32)


def shot_gradient(rows_res, rows_src):
    scale = 1.0 / rows_src.shape[-1]
    src_real = rows_src[:, 0]
    src_imag = rows_src[:, 1]
    stacked = jnp.stack(
        [jnp.stack([src_real, src_imag], axis=1), jnp.stack([-src_imag, src_real], axis=1)], axis=1
    )
    total = jnp.einsum("kyap,kxybp->kxab", rows_res, stacked, preferred_element_type=jnp.float32)
    return (-total * scale).astype(jnp.bfloat16)


def per_device(data, wavelet, panel_block, tiles, cover_rows, cover_freqs):
    freq_count = data.shape[0]
    block_rows = data.shape[2]
    shots = data.shape[3]
    slots = tiles.shape[0]
    peers = lax.axis_size("tiles")
    device = lax.axis_index("tiles")
    identity = (jnp.arange(block_rows)[:, None] == jnp.arange(shots)[None, :]).astype(jnp.float32)
    at_panel = (device == panel_block[0]).astype(jnp.float32)
    source_re = -data[:, 0].astype(jnp.float32) + at_panel * wavelet[:, 0, None, None] * identity
    source_im = -data[:, 1].astype(jnp.float32) + at_panel * wavelet[:, 1, None, None] * identity
    source = jnp.stack([source_re, source_im], axis=1).astype(jnp.bfloat16)
    slot_src = source[cover_freqs]
    earlier = jnp.arange(slots)[:, None] > jnp.arange(slots)[None, :]
    same_row = cover_rows[:, None] == cover_rows[None, :]
    position = jnp.sum(jnp.logical_and(same_row, earlier), axis=1)
    target = cover_rows * CAP + position
    freq_onehot = (cover_freqs[:, None] == jnp.arange(freq_count)[None, :]).astype(jnp.bfloat16)
    freq_values = jnp.arange(freq_count).astype(jnp.float32)

    def place(values):
        buffer = jnp.zeros((peers * CAP,) + values.shape[1:], values.dtype).at[target].set(values)
        return buffer.reshape((peers, CAP) + values.shape[1:])

    parts = complex_product(tiles, slot_src).astype(jnp.bfloat16)
    got_parts, got_freqs = (
        lax.all_to_all(place(parts), "tiles", split_axis=0, concat_axis=0, tiled=True),
        lax.all_to_all(place(freq_onehot), "tiles", split_axis=0, concat_axis=0, tiled=True),
    )
    predicted = jnp.einsum(
        "ncf,ncxbp->fxbp", got_freqs, got_parts, preferred_element_type=jnp.float32
    )
    residual = data.astype(jnp.float32) - predicted
    res_rounded = residual.astype(jnp.bfloat16)
    slot_index = jnp.sum(got_freqs.astype(jnp.float32) * freq_values[None, None, :], axis=2).astype(
        jnp.int32
    )
    send_back = res_rounded[slot_index]
    returned = lax.all_to_all(send_back, "tiles", split_axis=0, concat_axis=0, tiled=True)
    slot_res = returned.reshape((peers * CAP,) + returned.shape[2:])[target]
    gradient = shot_gradient(slot_res, slot_src)
    return (residual, gradient)


def solution(mesh):
    in_specs = (
        P("windows", None, "tiles", None),
        P(),
        P(),
        P(("windows", "tiles"), None, None, None),
        P(("windows", "tiles")),
        P(("windows", "tiles")),
    )
    out_specs = (P("windows", None, "tiles", None), P(("windows", "tiles"), None, None, None))
    return jax.shard_map(
        per_device, mesh=mesh, in_specs=in_specs, out_specs=out_specs, check_vma=False
    )
```

profile of v0, /device:TPU:15, one launch (start us, length us, event | category | flops | bytes accessed | tf_op | source)
XLA Modules:
  0.0 138.8 jit_solution(14115497230437427584)
XLA Ops:
  0.7 0.9 convert_reduce_fusion
  1.6 0.7 compare_select_fusion.2
  2.2 1.4 scatter_custom_fusion
  3.6 6.6 %all-to-all-start = ((bf16[16,2,8]{2,1,0:T(2,128)(2,1)}), bf16[16,2,8]{2,1,0:T(2,128)(2,1)S(1)}, u32[]{:S(2)}, u32[]{:S(2)}) async-start(bf16[16,2,8]{2,1,0:T(2,128)(2,1)} %bitcast), calls=%async_computation | async-start | bytes 16384 | tf_op jit(solution)/shard_map/all_to_all | solution.py:56
  10.2 0.7 compare_select_fusion.1
  11.5 1.3 slice_negate_fusion.1
  12.9 0.2 add_convert_fusion.1
  13.1 0.1 pad_maximum_fusion
  13.2 0.7 gather_fusion
  13.9 0.2 maximum_bitcast_fusion
  14.1 1.7 %bitcast_convert_fusion = bf16[16,2,128,128]{3,2,1,0:T(8,128)(2,1)} fusion(bf16[16,1,2,128,128]{4,3,2,1,0:T(8,128)(2,1)S(1)} %get-tuple-element.22, bf16[16,1,2,128,128]{4,3,2,1,0:T(8,128)(2,1)S(1)} %get-tuple-element.21, bf16[16,2,128,128]{3,2,1,0:T(8,128)(2,1)S(1)} %gather_fusion), kind=kOutput, calls=%fused_computation.16 | convolution fusion | flops 270008320 | bytes 4194304 | tf_op jit(solution)/shard_map/sxyab,sybp->sxap/dot_general | solution.py:15
  15.7 0.5 broadcast_in_dim.10
  16.2 2.3 %scatter_fusion = bf16[32,2,128,128]{3,2,1,0:T(8,128)(2,1)S(1)} fusion(bf16[32,2,128,128]{3,2,1,0:T(8,128)(2,1)S(1)} %broadcast_in_dim.10, s32[16]{0:T(128)S(1)} %compare_select_fusion.2, bf16[16,2,128,128]{3,2,1,0:T(8,128)(2,1)} %bitcast_convert_fusion), kind=kCustom, calls=%fused_computation.4 | custom fusion | bytes 3145792 | tf_op jit(solution)/shard_map/scatter | solution.py:50
  18.5 3.5 %copy.57 = bf16[16,2,2,128,128]{4,1,3,2,0:T(2,128)(2,1)} copy(bf16[16,2,2,128,128]{4,3,2,1,0:T(8,128)(2,1)S(1)} %bitcast.55) | data formatting | bytes 4194304 | tf_op jit(solution)/shard_map/reshape | solution.py:51
  22.0 6.0 %all-to-all-start.1 = ((bf16[16,2,2,128,128]{4,1,3,2,0:T(2,128)(2,1)}), bf16[16,2,2,128,128]{4,1,3,2,0:T(2,128)(2,1)S(1)}, u32[]{:S(2)}, u32[]{:S(2)}) async-start(bf16[16,2,2,128,128]{4,1,3,2,0:T(2,128)(2,1)} %copy.57), calls=%async_computation.1 | async-start | bytes 4194304 | tf_op jit(solution)/shard_map/all_to_all | solution.py:55
  28.1 0.1 multiply_reduce_fusion
  28.2 0.1 copy.74
  28.3 0.1 copy.62
  28.4 0.1 reshape.87
  28.5 47.0 %all-to-all-done.1 = bf16[16,2,2,128,128]{4,1,3,2,0:T(2,128)(2,1)S(1)} async-done(((bf16[16,2,2,128,128]{4,1,3,2,0:T(2,128)(2,1)}), bf16[16,2,2,128,128]{4,1,3,2,0:T(2,128)(2,1)S(1)}, u32[]{:S(2)}, u32[]{:S(2)}) %all-to-all-start.1) | async-done | bytes 2097184 | tf_op jit(solution)/shard_map/all_to_all | solution.py:55
  75.5 3.5 %fusion.37 = (bf16[8,2,128,128]{3,0,2,1:T(8,128)(2,1)S(1)}, f32[8,2,128,128]{3,0,2,1:T(8,128)}) fusion(bf16[16,2,2,128,128]{4,1,3,2,0:T(2,128)(2,1)S(1)} %all-to-all-done.1, bf16[16,2,8,1,1]{2,1,0,4,3:T(2,128)(2,1)S(1)} %bitcast.58, bf16[8,2,128,128]{3,2,1,0:T(8,128)(2,1)} %param.6), kind=kOutput, calls=%fused_computation.55 | convolution fusion | flops 17563648 | bytes 4194816 | tf_op jit(solution)/shard_map/ncf,ncxbp->fxbp/dot_general | solution.py:58
  79.0 0.1 copy.63
  79.1 2.2 %gather_fusion.1 = bf16[32,2,128,128]{3,2,1,0:T(8,128)(2,1)} fusion(bf16[8,2,128,128]{3,2,1,0:T(8,128)(2,1)S(1)} %copy.63, s32[1024]{0:T(1024)S(1)} %pad_clamp_fusion.1), kind=kCustom, calls=%fused_computation.1 | custom fusion | bytes 4194432 | tf_op jit(solution)/shard_map/gather | solution.py:66
  81.2 4.9 %all-to-all-start.2 = ((bf16[16,2,2,128,128]{4,3,2,1,0:T(8,128)(2,1)}), bf16[16,2,2,128,128]{4,3,2,1,0:T(8,128)(2,1)S(1)}, u32[]{:S(2)}, u32[]{:S(2)}) async-start(bf16[16,2,2,128,128]{4,3,2,1,0:T(8,128)(2,1)} %bitcast.19), calls=%async_computation.2 | async-start | bytes 4194304 | tf_op jit(solution)/shard_map/all_to_all | solution.py:67
  86.2 0.1 slice_negate_fusion
  86.3 1.1 maximum_bitcast_fusion.2
  87.4 0.2 copy-done
  87.6 1.2 copy.64
  88.7 44.8 %all-to-all-done.2 = bf16[16,2,2,128,128]{4,3,2,1,0:T(8,128)(2,1)S(1)} async-done(((bf16[16,2,2,128,128]{4,3,2,1,0:T(8,128)(2,1)}), bf16[16,2,2,128,128]{4,3,2,1,0:T(8,128)(2,1)S(1)}, u32[]{:S(2)}, u32[]{:S(2)}) %all-to-all-start.2) | async-done | bytes 2097184 | tf_op jit(solution)/shard_map/all_to_all | solution.py:67
  133.6 1.6 %gather_fusion.2 = bf16[16,2,128,128]{3,2,1,0:T(8,128)(2,1)} fusion(bf16[32,2,128,128]{3,2,1,0:T(8,128)(2,1)S(1)} %bitcast.56, s32[1024]{0:T(1024)S(1)} %pad_clamp_fusion), kind=kCustom, calls=%fused_computation.2 | custom fusion | bytes 2097216 | tf_op jit(solution)/shard_map/gather | solution.py:68
  135.2 2.2 %fusion.19 = bf16[16,2,128,128]{2,3,1,0:T(8,128)(2,1)S(1)} fusion(bf16[16,1,2,128,128]{4,3,2,1,0:T(8,128)(2,1)} %maximum_bitcast_fusion.2, bf16[16,1,2,128,128]{4,3,2,1,0:T(8,128)(2,1)S(1)} %bitcast.57, bf16[16,2,128,128]{3,2,1,0:T(8,128)(2,1)} %gather_fusion.2), kind=kOutput, calls=%fused_computation.20 | convolution fusion | flops 271056896 | bytes 4194304 | tf_op jit(solution)/shard_map/kyap,kxybp->kxab/dot_general | solution.py:25
  137.5 1.3 copy.65
  (14 shorter events, 0.1 us)
Async XLA Ops:
  0.6 12.2 %copy-start.2 = (f32[8,2]{0,1:T(2,128)S(1)}, f32[8,2]{0,1:T(2,128)}, u32[]{:S(2)}) copy-start(f32[8,2]{0,1:T(2,128)} %param.7) | copy-start | bytes 196
  0.6 12.2 %copy-start.1 = (bf16[8,2,128,128]{3,2,1,0:T(8,128)(2,1)S(1)}, bf16[8,2,128,128]{3,2,1,0:T(8,128)(2,1)}, u32[]{:S(2)}) copy-start(bf16[8,2,128,128]{3,2,1,0:T(8,128)(2,1)} %param.6) | copy-start | bytes 1572868
  3.6 18.5 %all-to-all-start = ((bf16[16,2,8]{2,1,0:T(2,128)(2,1)}), bf16[16,2,8]{2,1,0:T(2,128)(2,1)S(1)}, u32[]{:S(2)}, u32[]{:S(2)}) async-start(bf16[16,2,8]{2,1,0:T(2,128)(2,1)} %bitcast), calls=%async_computation | async-start | bytes 16384 | tf_op jit(solution)/shard_map/all_to_all | solution.py:56
  22.0 53.4 %all-to-all-start.1 = ((bf16[16,2,2,128,128]{4,1,3,2,0:T(2,128)(2,1)}), bf16[16,2,2,128,128]{4,1,3,2,0:T(2,128)(2,1)S(1)}, u32[]{:S(2)}, u32[]{:S(2)}) async-start(bf16[16,2,2,128,128]{4,1,3,2,0:T(2,128)(2,1)} %copy.57), calls=%async_computation.1 | async-start | bytes 4194304 | tf_op jit(solution)/shard_map/all_to_all | solution.py:55
  81.2 52.3 %all-to-all-start.2 = ((bf16[16,2,2,128,128]{4,3,2,1,0:T(8,128)(2,1)}), bf16[16,2,2,128,128]{4,3,2,1,0:T(8,128)(2,1)S(1)}, u32[]{:S(2)}, u32[]{:S(2)}) async-start(bf16[16,2,2,128,128]{4,3,2,1,0:T(8,128)(2,1)} %bitcast.19), calls=%async_computation.2 | async-start | bytes 4194304 | tf_op jit(solution)/shard_map/all_to_all | solution.py:67
  86.1 1.4 %copy-start = (f32[8,2,128,128]{3,0,2,1:T(8,128)S(1)}, f32[8,2,128,128]{3,0,2,1:T(8,128)}, u32[]{:S(2)}) copy-start(f32[8,2,128,128]{3,0,2,1:T(8,128)} %get-tuple-element.26) | copy-start | bytes 3145732
where the time goes:
time: 139 us
  waiting for transfers between devices  91.8 us (66%)
  starting transfers between devices  17.5 us (13%)
  local copies, waits for them, and re-layouts  13.9 us (10%)
  matrix products  7.41 us (5%)
  other arithmetic  6.69 us (5%)
  between operations  1.45 us (1%)
    all_to_all x1, waiting for transfers between devices, per_device(): lax.all_to_all(place(parts), 'tiles', split_axis=0, concat_axis=0, tiled=...  47 us
    all_to_all x1, waiting for transfers between devices, per_device(): lax.all_to_all(send_back, 'tiles', split_axis=0, concat_axis=0, tiled=True)  44.8 us
    all_to_all x1, starting transfers between devices, per_device(): lax.all_to_all(place(freq_onehot), 'tiles', split_axis=0, concat_axis=0,...  6.55 us
    all_to_all x1, starting transfers between devices, per_device(): lax.all_to_all(place(parts), 'tiles', split_axis=0, concat_axis=0, tiled=...  6.02 us
    all_to_all x1, starting transfers between devices, per_device(): lax.all_to_all(send_back, 'tiles', split_axis=0, concat_axis=0, tiled=True)  4.91 us
    reshape x1, local copies, waits for them, and re-layouts, place(): return buffer.reshape((peers, CAP) + values.shape[1:])  3.52 us
    dot_general x1, matrix products, per_device(): jnp.einsum('ncf,ncxbp->fxbp', got_freqs, got_parts, preferred_element_typ...  3.48 us
    unnamed x9, local copies, waits for them, and re-layouts  2.8 us
  transfers between devices with their start and end apart: 3, of which 2 were waited for; matrix products, arithmetic and copies ran while one was open for 10% of the time, Pallas kernels for 0%

commit v1 on v0

v1 whole, which is shorter than its diff:
```python
import functools

import jax
import jax.numpy as jnp
from jax import lax
from jax.experimental import pallas as pl
from jax.experimental.pallas import tpu as pltpu
from jax.sharding import PartitionSpec as P

CAP = 2
FAR, NEAR = 0, 1
F32, BF16 = jnp.float32, jnp.bfloat16


def kernel(
    n, wav_ref, panel_ref, rows_ref, freqs_ref, data_ref, tiles_ref, res_ref, grad_ref,
    src, tag_send, tag_recv, send, recv, part_sum, far_send, far_recv, res_bf, back_recv,
    back, ret, s_tag, r_tag, s_fwd, r_fwd, s_far, r_far, s_mid, r_mid, s_ret, r_ret,
):
    nf, _, nb, ns = data_ref.shape
    slots = tiles_ref.shape[0]
    half = n // 2
    me = lax.axis_index("tiles")
    base = (me // half) * half
    local = lax.rem(me, half)
    mirror = lax.rem(me + half, n)

    def ahead(k):
        return base + lax.rem(local + k, half)

    def behind(k):
        return base + lax.rem(local + half - k, half)

    def remote(src_ref, dst_ref, s_sem, r_sem, device):
        return pltpu.make_async_remote_copy(
            src_ref=src_ref, dst_ref=dst_ref, send_sem=s_sem, recv_sem=r_sem,
            device_id={"tiles": device}, device_id_type=pl.DeviceIdType.MESH,
        )

    def tag_copy(k):
        return remote(tag_send.at[k], tag_recv.at[k], s_tag.at[k], r_tag.at[k], ahead(k))

    def fwd_copy(k, side, g):
        return remote(send.at[k, side, g], recv.at[k, side, g],
                      s_fwd.at[k, side, g], r_fwd.at[k, side, g], ahead(k))

    def far_copy(f, g):
        return remote(far_send.at[f, g], far_recv.at[f, g], s_far.at[f, g], r_far.at[f, g], mirror)

    def mid_copy(f, g):
        return remote(res_bf.at[f, g], back_recv.at[f, g], s_mid.at[f, g], r_mid.at[f, g], mirror)

    def ret_copy(k, side, g):
        return remote(back.at[k, side, g], ret.at[k, side, g],
                      s_ret.at[k, side, g], r_ret.at[k, side, g], behind(k))

    def loop(lo, hi, body):
        def step(i, carry):
            body(i)
            return carry
        lax.fori_loop(lo, hi, step, 0)

    barrier = pltpu.get_barrier_semaphore()

    def greet(k):
        pl.semaphore_signal(barrier, inc=1, device_id={"tiles": ahead(k)},
                            device_id_type=pl.DeviceIdType.MESH)
    loop(1, half, greet)
    pl.semaphore_signal(barrier, inc=1, device_id={"tiles": mirror},
                        device_id_type=pl.DeviceIdType.MESH)

    eye = lax.broadcasted_iota(jnp.int32, (nb, ns), 0) == lax.broadcasted_iota(jnp.int32, (nb, ns), 1)
    at_panel = jnp.where(me == panel_ref[0], 1.0, 0.0).astype(F32)

    def make_source(f):
        re = jnp.where(eye, at_panel * wav_ref[f, 0], 0.0) - data_ref[f, 0].astype(F32)
        im = jnp.where(eye, at_panel * wav_ref[f, 1], 0.0) - data_ref[f, 1].astype(F32)
        re, im = re.astype(BF16), im.astype(BF16)
        src[f, :nb, :ns] = re
        src[f, :nb, ns:] = im
        src[f, nb:, :ns] = -im
        src[f, nb:, ns:] = re
    loop(0, nf, make_source)

    def find(row):
        first = jnp.int32(-1)
        second = jnp.int32(-1)
        for t in reversed(range(slots)):
            hit = rows_ref[t] == row
            second = jnp.where(hit, first, second)
            first = jnp.where(hit, jnp.int32(t), first)
        return first, second

    def make_parts(k, side):
        row = ahead(k)
        if side == FAR:
            row = lax.rem(row + half, n)
        for c, t in enumerate(find(row)):
            at = jnp.maximum(t, 0)
            freq = freqs_ref[at]
            tag = jnp.where(t >= 0, freq, -1).astype(F32)
            tag_send[k, side * CAP + c : side * CAP + c + 1, :] = jnp.full((1, ns), tag, F32)
            left = jnp.concatenate([tiles_ref[at, 0], tiles_ref[at, 1]], axis=1)
            part = jnp.dot(left, src[freq], preferred_element_type=F32).astype(BF16)
            send[k, side, 0, c] = part[:, :ns]
            send[k, side, 1, c] = part[:, ns:]

    pl.semaphore_wait(barrier, half)

    def send_far(k):
        make_parts(k, FAR)
        fwd_copy(k, FAR, 0).start()
    loop(1, half, send_far)

    def send_far_rest(k):
        fwd_copy(k, FAR, 1).start()
    loop(1, half, send_far_rest)

    def send_near(k):
        make_parts(k, NEAR)
        tag_copy(k).start()
        fwd_copy(k, NEAR, 0).start()
        fwd_copy(k, NEAR, 1).start()
    loop(1, half, send_near)
    make_parts(0, FAR)
    make_parts(0, NEAR)

    def wait_tag(k):
        tag_copy(k).wait()
    loop(1, half, wait_tag)

    def gathered(side, f, g):
        want = f.astype(F32)

        def add(tags, parts, k, acc):
            for c in range(CAP):
                tag = tags[k, side * CAP + c : side * CAP + c + 1, :]
                acc = acc + jnp.where(tag == want, parts[k, side, g, c].astype(F32), 0.0)
            return acc
        acc = add(tag_send, send, 0, jnp.zeros((nb, ns), F32))
        return lax.fori_loop(1, half, functools.partial(add, tag_recv, recv), acc)

    def wait_fwd(side, g):
        def body(k):
            fwd_copy(k, side, g).wait()
        loop(1, half, body)

    for g in range(2):
        wait_fwd(FAR, g)

        def sum_far(f, g=g):
            far_send[f, g] = gathered(FAR, f, g).astype(BF16)
            far_copy(f, g).start()
        loop(0, nf, sum_far)
    for g in range(2):
        wait_fwd(NEAR, g)

        def sum_near(f, g=g):
            part_sum[f, g] = data_ref[f, g].astype(F32) - gathered(NEAR, f, g)
        loop(0, nf, sum_near)

    def give_back(side, g, rows):
        def pick(tags, k, out):
            for c in range(CAP):
                tag = tags[k, side * CAP + c : side * CAP + c + 1, :]
                value = rows[0, g].astype(F32)
                for f in range(1, nf):
                    value = jnp.where(tag == float(f), rows[f, g].astype(F32), value)
                out[k, side, g, c] = value.astype(BF16)

        def body(k):
            pick(tag_recv, k, back)
            ret_copy(k, side, g).start()
        loop(1, half, body)
        pick(tag_send, 0, ret)

    for g in range(2):
        def finish(f, g=g):
            far_copy(f, g).wait()
            value = part_sum[f, g] - far_recv[f, g].astype(F32)
            res_ref[f, g] = value
            res_bf[f, g] = value.astype(BF16)
            mid_copy(f, g).start()
        loop(0, nf, finish)
        give_back(NEAR, g, res_bf)
    for g in range(2):
        def wait_mid(f, g=g):
            mid_copy(f, g).wait()
        loop(0, nf, wait_mid)
        give_back(FAR, g, back_recv)

    def wait_ret(k):
        for side in range(2):
            for g in range(2):
                ret_copy(k, side, g).wait()
    loop(1, half, wait_ret)

    scale = 1.0 / ns

    def make_gradient(t):
        row = rows_ref[t]
        position = jnp.int32(0)
        for other in range(slots):
            same = jnp.logical_and(rows_ref[other] == row, other < t)
            position = jnp.where(same, jnp.int32(1), position)
        side = jnp.where(jnp.logical_and(row >= base, row < base + half), NEAR, FAR)
        k = lax.rem(row + n - local, half)
        left = jnp.concatenate([ret[k, side, 0, position], ret[k, side, 1, position]], axis=1)
        out = lax.dot_general(left, src[freqs_ref[t]], (((1,), (1,)), ((), ())),
                              preferred_element_type=F32)
        out = (-out * scale).astype(BF16)
        grad_ref[t, 0] = out[:, :nb]
        grad_ref[t, 1] = out[:, nb:]
    loop(0, slots, make_gradient)


def per_device(data, wavelet, panel_block, tiles, cover_rows, cover_freqs):
    nf, _, nb, ns = data.shape
    n = lax.axis_size("tiles")
    half = n // 2
    dma = pltpu.SemaphoreType.DMA
    smem = pl.BlockSpec(memory_space=pltpu.SMEM)
    vmem = pl.BlockSpec(memory_space=pltpu.VMEM)
    parcels = pltpu.VMEM((half, 2, 2, CAP, nb, ns), BF16)
    panel = pltpu.VMEM((nf, 2, nb, ns), BF16)
    return pl.pallas_call(
        functools.partial(kernel, n),
        out_shape=(
            jax.ShapeDtypeStruct(data.shape, F32),
            jax.ShapeDtypeStruct(tiles.shape, BF16),
        ),
        in_specs=[smem] * 4 + [vmem] * 2,
        out_specs=(vmem, vmem),
        scratch_shapes=[
            pltpu.VMEM((nf, 2 * nb, 2 * ns), BF16),
            pltpu.VMEM((half, 8, ns), F32),
            pltpu.VMEM((half, 8, ns), F32),
            parcels,
            parcels,
            pltpu.VMEM((nf, 2, nb, ns), F32),
            panel,
            panel,
            panel,
            panel,
            parcels,
            parcels,
            dma((half,)), dma((half,)),
            dma((half, 2, 2)), dma((half, 2, 2)),
            dma((nf, 2)), dma((nf, 2)),
            dma((nf, 2)), dma((nf, 2)),
            dma((half, 2, 2)), dma((half, 2, 2)),
        ],
        compiler_params=pltpu.CompilerParams(
            collective_id=0, has_side_effects=True, vmem_limit_bytes=60 * 1024 * 1024
        ),
    )(wavelet, panel_block, cover_rows, cover_freqs, data, tiles)


def solution(mesh):
    in_specs = (
        P("windows", None, "tiles", None),
        P(),
        P(),
        P(("windows", "tiles"), None, None, None),
        P(("windows", "tiles")),
        P(("windows", "tiles")),
    )
    out_specs = (P("windows", None, "tiles", None), P(("windows", "tiles"), None, None, None))
    return jax.shard_map(
        per_device, mesh=mesh, in_specs=in_specs, out_specs=out_specs, check_vma=False
    )
```

time: 139 us -> 103 us (0.74)
  the two profiles are of different devices: /device:TPU:15 before, /device:TPU:0 now
where the time goes in v1:
time: 103 us
  Pallas kernels  97.2 us (94%)
  local copies, waits for them, and re-layouts  4.04 us (4%)
  between operations  1.31 us (1%)
    pallas_call x1, Pallas kernels, per_device(): pl.pallas_call(functools.partial(kernel, n), out_shape=(jax.ShapeDtypeStr...  97.2 us
    unnamed x7, local copies, waits for them, and re-layouts  4.04 us

profile of v1, /device:TPU:0, one launch (start us, length us, event | category | flops | bytes accessed | tf_op | source)
XLA Modules:
  0.0 102.5 jit_solution(11226908468411948894)
XLA Ops:
  0.6 0.0 copy-start.1
  1.3 0.0 copy-done.1
  1.3 0.7 copy.8.wav_ref
  2.0 97.2 %shard_map.77 = (f32[8,2,128,128]{3,2,1,0:T(8,128)}, bf16[16,2,128,128]{3,2,1,0:T(8,128)(2,1)}) custom-call(f32[8,2]{1,0:T(8,128)} %copy.8.wav_ref, s32[1]{0:T(128)S(6)} %copy.11.panel_ref, s32[16]{0:T(128)} %rows_ref.1, s32[16]{0:T(128)} %freqs_ref.1, bf16[8,2,128,128]{3,2,1,0:T(8,128)(2,1)} %data_ref.1, bf16[16,2,128,128]{3,2,1,0:T(8,128)(2,1)} %tiles_ref.1), custom_call_target="tpu_custom_call" | custom-call | tf_op jit(solution)/shard_map/pallas_call | solution.py:226
  99.2 0.0 copy-start
  99.2 2.4 %copy.12 = f32[8,2,128,128]{3,2,1,0:T(8,128)} copy(f32[8,2,128,128]{3,2,1,0:T(8,128)} %get-tuple-element.4) | data formatting | bytes 2097152
  101.5 0.0 copy-done
  101.5 1.0 copy.13
Async XLA Ops:
  0.6 0.7 copy-start.1
  99.2 2.4 %copy-start = (bf16[16,2,128,128]{3,2,1,0:T(8,128)(2,1)S(1)}, bf16[16,2,128,128]{3,2,1,0:T(8,128)(2,1)}, u32[]{:S(2)}) copy-start(bf16[16,2,128,128]{3,2,1,0:T(8,128)(2,1)} %get-tuple-element.5) | copy-start | bytes 3145732

commit v2 on v1

v2 whole, which is shorter than its diff:
```python
import functools

import jax
import jax.numpy as jnp
from jax import lax
from jax.experimental import pallas as pl
from jax.experimental.pallas import tpu as pltpu
from jax.sharding import PartitionSpec as P

CAP = 2
GROUPS = 4
UP, DOWN = 0, 1
F32, BF16 = jnp.float32, jnp.bfloat16


def kernel(
    n, wav_ref, panel_ref, rows_ref, freqs_ref, data_ref, tiles_ref, res_ref, grad_ref,
    src, found, tag_send, tag_recv, send, recv, hop_send, hop_recv, rows_bf, back, ret,
    s_tag, r_tag, s_fwd, r_fwd, s_hop, r_hop, s_row, r_row, s_ret, r_ret,
):
    nf, _, nb, ns = data_ref.shape
    slots = tiles_ref.shape[0]
    width = n // GROUPS
    last = GROUPS - 1
    me = lax.axis_index("tiles")
    z = me // width
    local = lax.rem(me, width)

    def ahead(k):
        return z * width + lax.rem(local + k, width)

    def behind(k):
        return z * width + lax.rem(local + width - k, width)

    def remote(src_ref, dst_ref, s_sem, r_sem, device):
        return pltpu.make_async_remote_copy(
            src_ref=src_ref, dst_ref=dst_ref, send_sem=s_sem, recv_sem=r_sem,
            device_id={"tiles": device}, device_id_type=pl.DeviceIdType.MESH,
        )

    def tag_copy(k):
        return remote(tag_send.at[k], tag_recv.at[k], s_tag.at[k], r_tag.at[k], ahead(k))

    def fwd_copy(k, r, g):
        return remote(send.at[k, r, g], recv.at[k, r, g],
                      s_fwd.at[k, r, g], r_fwd.at[k, r, g], ahead(k))

    def next_device(way):
        return me + width if way == UP else me - width

    def hop_copy(way, r, f, g):
        return remote(hop_send.at[r, g, f], hop_recv.at[way, r, g, f],
                      s_hop.at[r, g, f], r_hop.at[way, r, g, f], next_device(way))

    def row_copy(way, r, f, g):
        return remote(rows_bf.at[r, g, f], rows_bf.at[r, g, f],
                      s_row.at[way, r, g, f], r_row.at[r, g, f], next_device(way))

    def ret_copy(k, r, g):
        return remote(back.at[k, r, g], ret.at[k, r, g],
                      s_ret.at[k, r, g], r_ret.at[k, r, g], behind(k))

    def loop(lo, hi, body):
        def step(i, carry):
            body(i)
            return carry
        lax.fori_loop(lo, hi, step, 0)

    barrier = pltpu.get_barrier_semaphore()

    def greet(device):
        pl.semaphore_signal(barrier, inc=1, device_id={"tiles": device},
                            device_id_type=pl.DeviceIdType.MESH)
    loop(1, width, lambda k: greet(ahead(k)))

    @pl.when(z < last)
    def _():
        greet(me + width)

    @pl.when(z > 0)
    def _():
        greet(me - width)

    eye = lax.broadcasted_iota(jnp.int32, (nb, ns), 0) == lax.broadcasted_iota(jnp.int32, (nb, ns), 1)
    at_panel = jnp.where(me == panel_ref[0], 1.0, 0.0).astype(F32)

    def make_source(f):
        re = jnp.where(eye, at_panel * wav_ref[f, 0], 0.0) - data_ref[f, 0].astype(F32)
        im = jnp.where(eye, at_panel * wav_ref[f, 1], 0.0) - data_ref[f, 1].astype(F32)
        re, im = re.astype(BF16), im.astype(BF16)
        src[f, :nb, :ns] = re
        src[f, :nb, ns:] = im
        src[f, nb:, :ns] = -im
        src[f, nb:, ns:] = re
    loop(0, nf, make_source)

    def find(k):
        for r in range(GROUPS):
            row = r * width + lax.rem(local + k, width)
            first = jnp.int32(-1)
            second = jnp.int32(-1)
            for t in reversed(range(slots)):
                hit = rows_ref[t] == row
                second = jnp.where(hit, first, second)
                first = jnp.where(hit, jnp.int32(t), first)
            for c, t in enumerate((first, second)):
                found[(k * GROUPS + r) * CAP + c] = jnp.maximum(t, 0)
                tag = jnp.where(t >= 0, freqs_ref[jnp.maximum(t, 0)], -1).astype(F32)
                tag_send[k, r * CAP + c : r * CAP + c + 1, :] = jnp.full((1, ns), tag, F32)
    loop(0, width, find)

    def make_parts(k, r):
        for c in range(CAP):
            at = found[(k * GROUPS + r) * CAP + c]
            left = jnp.concatenate([tiles_ref[at, 0], tiles_ref[at, 1]], axis=1)
            part = jnp.dot(left, src[freqs_ref[at]], preferred_element_type=F32).astype(BF16)
            send[k, r, 0, c] = part[:, :ns]
            send[k, r, 1, c] = part[:, ns:]

    order = []
    for i in range(GROUPS):
        options = ORDERS[i]
        value = jnp.int32(options[0])
        for at in range(1, GROUPS):
            value = jnp.where(z == at, jnp.int32(options[at]), value)
        order.append(value)

    pl.semaphore_wait(barrier, width - 1 + jnp.where(z > 0, 1, 0) + jnp.where(z < last, 1, 0))
    loop(1, width, lambda k: tag_copy(k).start())

    for r in order:
        def send_parts(k, r=r):
            make_parts(k, r)
            fwd_copy(k, r, 0).start()
            fwd_copy(k, r, 1).start()
        loop(1, width, send_parts)
        make_parts(0, r)
    loop(1, width, lambda k: tag_copy(k).wait())

    def gathered(r, f, g):
        want = f.astype(F32)

        def add(tags, parts, k, acc):
            for c in range(CAP):
                tag = tags[k, pl.ds(r * CAP + c, 1), :]
                acc = acc + jnp.where(tag == want, parts[k, r, g, c].astype(F32), 0.0)
            return acc
        acc = add(tag_send, send, 0, jnp.zeros((nb, ns), F32))
        return lax.fori_loop(1, width, functools.partial(add, tag_recv, recv), acc,
                             unroll=width <= 4)

    for r in order[:-1]:
        for g in range(2):
            loop(1, width, lambda k: fwd_copy(k, r, g).wait_recv())
            for way in (UP, DOWN):
                @pl.when(r > z if way == UP else r < z)
                def _(r=r, g=g, way=way):
                    inner = z > 0 if way == UP else z < last

                    @pl.when(inner)
                    def _():
                        def add_on(f):
                            acc = gathered(r, f, g)
                            hop_copy(way, r, f, g).wait_recv()
                            acc = acc + hop_recv[way, r, g, f].astype(F32)
                            hop_send[r, g, f] = acc.astype(BF16)
                            hop_copy(way, r, f, g).start()
                        loop(0, nf, add_on)

                    @pl.when(jnp.logical_not(inner))
                    def _():
                        def begin(f):
                            hop_send[r, g, f] = gathered(r, f, g).astype(BF16)
                            hop_copy(way, r, f, g).start()
                        loop(0, nf, begin)

    for g in range(2):
        loop(1, width, lambda k: fwd_copy(k, z, g).wait_recv())

        def subtract(f, g=g):
            res_ref[f, g] = data_ref[f, g].astype(F32) - gathered(z, f, g)
        loop(0, nf, subtract)

    def give_back(r, g):
        def pick(tags, k, out):
            for c in range(CAP):
                tag = tags[k, pl.ds(r * CAP + c, 1), :]
                value = rows_bf[r, g, 0].astype(F32)
                for f in range(1, nf):
                    value = jnp.where(tag == float(f), rows_bf[r, g, f].astype(F32), value)
                out[k, r, g, c] = value.astype(BF16)

        def body(k):
            pick(tag_recv, k, back)
            ret_copy(k, r, g).start()
        loop(1, width, body)
        pick(tag_send, 0, ret)

    for g in range(2):
        def finish(f, g=g):
            @pl.when(z > 0)
            def _():
                hop_copy(UP, z, f, g).wait_recv()
                res_ref[f, g] = res_ref[f, g] - hop_recv[UP, z, g, f].astype(F32)

            @pl.when(z < last)
            def _():
                hop_copy(DOWN, z, f, g).wait_recv()
                res_ref[f, g] = res_ref[f, g] - hop_recv[DOWN, z, g, f].astype(F32)
            rows_bf[z, g, f] = res_ref[f, g].astype(BF16)

            @pl.when(z < last)
            def _():
                row_copy(UP, z, f, g).start()

            @pl.when(z > 0)
            def _():
                row_copy(DOWN, z, f, g).start()
        loop(0, nf, finish)

    arrivals = []
    for i in range(GROUPS - 1):
        options = ARRIVALS[i]
        value = jnp.int32(options[0])
        for at in range(1, GROUPS):
            value = jnp.where(z == at, jnp.int32(options[at]), value)
        arrivals.append(value)

    for g in range(2):
        give_back(z, g)
    for r in arrivals:
        for g in range(2):
            def pass_on(f, r=r, g=g):
                row_copy(UP, r, f, g).wait_recv()

                @pl.when(jnp.logical_and(r < z, z < last))
                def _():
                    row_copy(UP, r, f, g).start()

                @pl.when(jnp.logical_and(r > z, z > 0))
                def _():
                    row_copy(DOWN, r, f, g).start()
            loop(0, nf, pass_on)
            give_back(r, g)

    for r in range(GROUPS):
        for g in range(2):
            loop(1, width, lambda k: ret_copy(k, r, g).wait_recv())

    scale = 1.0 / ns

    def make_gradient(t):
        row = rows_ref[t]
        position = jnp.int32(0)
        for other in range(slots):
            same = jnp.logical_and(rows_ref[other] == row, other < t)
            position = jnp.where(same, jnp.int32(1), position)
        r = row // width
        k = lax.rem(row + width - local, width)
        left = jnp.concatenate([ret[k, r, 0, position], ret[k, r, 1, position]], axis=1)
        out = lax.dot_general(left, src[freqs_ref[t]], (((1,), (1,)), ((), ())),
                              preferred_element_type=F32)
        out = (-out * scale).astype(BF16)
        grad_ref[t, 0] = out[:, :nb]
        grad_ref[t, 1] = out[:, nb:]
    loop(0, slots, make_gradient)

    for r in range(GROUPS):
        for g in range(2):
            def sent(k, r=r, g=g):
                fwd_copy(k, r, g).wait_send()
                ret_copy(k, r, g).wait_send()
            loop(1, width, sent)

            def hopped(f, r=r, g=g):
                @pl.when(r != z)
                def _():
                    hop_copy(UP, r, f, g).wait_send()

                @pl.when(jnp.logical_and(r <= z, z < last))
                def _():
                    row_copy(UP, r, f, g).wait_send()

                @pl.when(jnp.logical_and(r >= z, z > 0))
                def _():
                    row_copy(DOWN, r, f, g).wait_send()
            loop(0, nf, hopped)


ORDERS = ((3, 3, 0, 0), (2, 0, 3, 1), (1, 2, 1, 2), (0, 1, 2, 3))
ARRIVALS = ((1, 0, 3, 2), (2, 2, 1, 1), (3, 3, 0, 0))


def per_device(data, wavelet, panel_block, tiles, cover_rows, cover_freqs):
    nf, _, nb, ns = data.shape
    n = lax.axis_size("tiles")
    width = n // GROUPS
    dma = pltpu.SemaphoreType.DMA
    smem = pl.BlockSpec(memory_space=pltpu.SMEM)
    vmem = pl.BlockSpec(memory_space=pltpu.VMEM)
    parcels = pltpu.VMEM((width, GROUPS, 2, CAP, nb, ns), BF16)
    tags = pltpu.VMEM((width, GROUPS * CAP, ns), F32)
    panels = (GROUPS, 2, nf)
    return pl.pallas_call(
        functools.partial(kernel, n),
        out_shape=(
            jax.ShapeDtypeStruct(data.shape, F32),
            jax.ShapeDtypeStruct(tiles.shape, BF16),
        ),
        in_specs=[smem] * 4 + [vmem] * 2,
        out_specs=(vmem, vmem),
        scratch_shapes=[
            pltpu.VMEM((nf, 2 * nb, 2 * ns), BF16),
            pltpu.SMEM((n * CAP,), jnp.int32),
            tags,
            tags,
            parcels,
            parcels,
            pltpu.VMEM(panels + (nb, ns), BF16),
            pltpu.VMEM((2,) + panels + (nb, ns), BF16),
            pltpu.VMEM(panels + (nb, ns), BF16),
            parcels,
            parcels,
            dma((width,)), dma((width,)),
            dma((width, GROUPS, 2)), dma((width, GROUPS, 2)),
            dma(panels), dma((2,) + panels),
            dma((2,) + panels), dma(panels),
            dma((width, GROUPS, 2)), dma((width, GROUPS, 2)),
        ],
        compiler_params=pltpu.CompilerParams(
            collective_id=0, has_side_effects=True, vmem_limit_bytes=60 * 1024 * 1024
        ),
    )(wavelet, panel_block, cover_rows, cover_freqs, data, tiles)


def solution(mesh):
    in_specs = (
        P("windows", None, "tiles", None),
        P(),
        P(),
        P(("windows", "tiles"), None, None, None),
        P(("windows", "tiles")),
        P(("windows", "tiles")),
    )
    out_specs = (P("windows", None, "tiles", None), P(("windows", "tiles"), None, None, None))
    return jax.shard_map(
        per_device, mesh=mesh, in_specs=in_specs, out_specs=out_specs, check_vma=False
    )
```

time: 103 us -> 98.7 us (0.958)
  Pallas kernels: 97.2 us -> 93.2 us
    pallas_call x1, Pallas kernels: 97.2 us -> 93.2 us  [per_device(): pl.pallas_call(functools.partial(kernel, n), out_shape=(jax.ShapeDtypeStr...]
where the time goes in v2:
time: 98.7 us; the launch traced here: 98.6 us
  Pallas kernels  93.2 us (94%)
  local copies, waits for them, and re-layouts  4.04 us (4%)
  between operations  1.31 us (1%)
    pallas_call x1, Pallas kernels, per_device(): pl.pallas_call(functools.partial(kernel, n), out_shape=(jax.ShapeDtypeStr...  93.2 us
    unnamed x7, local copies, waits for them, and re-layouts  4.04 us

profile of v2, /device:TPU:0, one launch (start us, length us, event | category | flops | bytes accessed | tf_op | source)
XLA Modules:
  0.0 98.6 jit_solution(14651222621026071675)
XLA Ops:
  0.6 0.0 copy-start.1
  1.3 0.0 copy-done.1
  1.3 0.7 copy.8.wav_ref
  2.0 93.2 %shard_map.77 = (f32[8,2,128,128]{3,2,1,0:T(8,128)}, bf16[16,2,128,128]{3,2,1,0:T(8,128)(2,1)}) custom-call(f32[8,2]{1,0:T(8,128)} %copy.8.wav_ref, s32[1]{0:T(128)S(6)} %copy.11.panel_ref, s32[16]{0:T(128)} %rows_ref.1, s32[16]{0:T(128)} %freqs_ref.1, bf16[8,2,128,128]{3,2,1,0:T(8,128)(2,1)} %data_ref.1, bf16[16,2,128,128]{3,2,1,0:T(8,128)(2,1)} %tiles_ref.1), custom_call_target="tpu_custom_call" | custom-call | tf_op jit(solution)/shard_map/pallas_call | solution.py:304
  95.2 0.0 copy-start
  95.2 2.4 %copy.12 = f32[8,2,128,128]{3,2,1,0:T(8,128)} copy(f32[8,2,128,128]{3,2,1,0:T(8,128)} %get-tuple-element.4) | data formatting | bytes 2097152
  97.6 0.0 copy-done
  97.6 1.0 copy.13
Async XLA Ops:
  0.6 0.7 copy-start.1
  95.2 2.4 %copy-start = (bf16[16,2,128,128]{3,2,1,0:T(8,128)(2,1)S(1)}, bf16[16,2,128,128]{3,2,1,0:T(8,128)(2,1)}, u32[]{:S(2)}) copy-start(bf16[16,2,128,128]{3,2,1,0:T(8,128)(2,1)} %get-tuple-element.5) | copy-start | bytes 3145732

commit v3 on v2

--- a/solution.py
+++ b/solution.py
@@ -10,6 +10,7 @@
 CAP = 2
 GROUPS = 4
 UP, DOWN = 0, 1
+LAG = 4
 F32, BF16 = jnp.float32, jnp.bfloat16
 
 
@@ -46,7 +47,7 @@
                       s_fwd.at[k, r, g], r_fwd.at[k, r, g], ahead(k))
 
     def next_device(way):
-        return me + width if way == UP else me - width
+        return me + width * (1 - 2 * way)
 
     def hop_copy(way, r, f, g):
         return remote(hop_send.at[r, g, f], hop_recv.at[way, r, g, f],
@@ -117,18 +118,18 @@
             send[k, r, 0, c] = part[:, :ns]
             send[k, r, 1, c] = part[:, ns:]
 
-    order = []
-    for i in range(GROUPS):
-        options = ORDERS[i]
-        value = jnp.int32(options[0])
-        for at in range(1, GROUPS):
-            value = jnp.where(z == at, jnp.int32(options[at]), value)
-        order.append(value)
+    low = z < GROUPS // 2
+    inward = jnp.where(low, UP, DOWN)
+    outward = 1 - inward
+    outer = jnp.logical_or(z == 0, z == last)
+
+    def group(c):
+        return jnp.where(low, c, last - c)
 
     pl.semaphore_wait(barrier, width - 1 + jnp.where(z > 0, 1, 0) + jnp.where(z < last, 1, 0))
     loop(1, width, lambda k: tag_copy(k).start())
 
-    for r in order:
+    for r in (group(3), group(0), group(2), group(1)):
         def send_parts(k, r=r):
             make_parts(k, r)
             fwd_copy(k, r, 0).start()
@@ -149,37 +150,30 @@
         return lax.fori_loop(1, width, functools.partial(add, tag_recv, recv), acc,
                              unroll=width <= 4)
 
-    for r in order[:-1]:
-        for g in range(2):
-            loop(1, width, lambda k: fwd_copy(k, r, g).wait_recv())
-            for way in (UP, DOWN):
-                @pl.when(r > z if way == UP else r < z)
-                def _(r=r, g=g, way=way):
-                    inner = z > 0 if way == UP else z < last
-
-                    @pl.when(inner)
-                    def _():
-                        def add_on(f):
-                            acc = gathered(r, f, g)
-                            hop_copy(way, r, f, g).wait_recv()
-                            acc = acc + hop_recv[way, r, g, f].astype(F32)
-                            hop_send[r, g, f] = acc.astype(BF16)
-                            hop_copy(way, r, f, g).start()
-                        loop(0, nf, add_on)
-
-                    @pl.when(jnp.logical_not(inner))
-                    def _():
-                        def begin(f):
-                            hop_send[r, g, f] = gathered(r, f, g).astype(BF16)
-                            hop_copy(way, r, f, g).start()
-                        loop(0, nf, begin)
-
-    for g in range(2):
-        loop(1, width, lambda k: fwd_copy(k, z, g).wait_recv())
-
-        def subtract(f, g=g):
-            res_ref[f, g] = data_ref[f, g].astype(F32) - gathered(z, f, g)
-        loop(0, nf, subtract)
+    pieces = 2 * nf
+
+    def wait_plane(r, g):
+        loop(1, width, lambda k: fwd_copy(k, r, g).wait_recv())
+
+    def arrived(way, r, f, g):
+        hop_copy(way, r, f, g).wait_recv()
+        return hop_recv[way, r, g, f].astype(F32)
+
+    def begin(r, f, g):
+        hop_send[r, g, f] = gathered(r, f, g).astype(BF16)
+        hop_copy(inward, r, f, g).start()
+
+    def add_on(way, r, f, g):
+        acc = gathered(r, f, g) + arrived(way, r, f, g)
+        hop_send[r, g, f] = acc.astype(BF16)
+        hop_copy(way, r, f, g).start()
+
+    def pass_on(way, r, f, g):
+        row_copy(way, r, f, g).wait_recv()
+        row_copy(way, r, f, g).start()
+
+    def wait_row(r, g):
+        loop(0, nf, lambda f: row_copy(UP, r, f, g).wait_recv())
 
     def give_back(r, g):
         def pick(tags, k, out):
@@ -196,52 +190,86 @@
         loop(1, width, body)
         pick(tag_send, 0, ret)
 
-    for g in range(2):
-        def finish(f, g=g):
-            @pl.when(z > 0)
+    @pl.when(outer)
+    def _():
+        for g in range(2):
+            wait_plane(group(3), g)
+            loop(0, nf, lambda f: begin(group(3), f, g))
+        for g in range(2):
+            wait_plane(z, g)
+
+            def finish(f, g=g):
+                value = data_ref[f, g].astype(F32) - gathered(z, f, g)
+                value = value - arrived(outward, z, f, g)
+                res_ref[f, g] = value
+                rows_bf[z, g, f] = value.astype(BF16)
+                row_copy(inward, z, f, g).start()
+            loop(0, nf, finish)
+        for g in range(2):
+            wait_plane(group(2), g)
+            wait_plane(group(1), g)
+
+            def begin_two(f, g=g):
+                begin(group(2), f, g)
+                begin(group(1), f, g)
+            loop(0, nf, begin_two)
+        give_back(z, 0)
+        give_back(z, 1)
+        for g in range(2):
+            wait_row(group(3), g)
+            give_back(group(3), g)
+        for g in range(2):
+            for c in (1, 2):
+                wait_row(group(c), g)
+                give_back(group(c), g)
+
+    @pl.when(jnp.logical_not(outer))
+    def _():
+        def end_row(f, g):
+            value = data_ref[f, g].astype(F32) - gathered(z, f, g)
+            value = value - arrived(UP, z, f, g) - arrived(DOWN, z, f, g)
+            res_ref[f, g] = value
+            rows_bf[z, g, f] = value.astype(BF16)
+            row_copy(inward, z, f, g).start()
+            row_copy(outward, z, f, g).start()
+
+        tasks = (
+            (0, lambda f, g: add_on(inward, group(3), f, g)),
+            (LAG, lambda f, g: add_on(outward, group(0), f, g)),
+            (pieces, lambda f, g: pass_on(inward, group(0), f, g)),
+            (pieces + LAG, lambda f, g: pass_on(outward, group(3), f, g)),
+            (2 * pieces, lambda f, g: add_on(inward, group(2), f, g)),
+            (2 * pieces + LAG, end_row),
+            (2 * pieces + 2 * LAG, lambda f, g: pass_on(outward, group(2), f, g)),
+        )
+        handed = (
+            (2 * pieces + 2, 0, 0), (2 * pieces + 4, 0, 1),
+            (2 * pieces + LAG + 1, 3, 0), (2 * pieces + LAG + 3, 3, 1),
+            (2 * pieces + LAG + nf, 1, 0), (2 * pieces + 2 * LAG + nf, 2, 0),
+            (3 * pieces + LAG, 1, 1),
+        )
+        for g in range(2):
+            wait_plane(group(3), g)
+            wait_plane(group(0), g)
+
+        def step(i):
+            @pl.when(i == 2 * pieces)
             def _():
-                hop_copy(UP, z, f, g).wait_recv()
-                res_ref[f, g] = res_ref[f, g] - hop_recv[UP, z, g, f].astype(F32)
-
-            @pl.when(z < last)
-            def _():
-                hop_copy(DOWN, z, f, g).wait_recv()
-                res_ref[f, g] = res_ref[f, g] - hop_recv[DOWN, z, g, f].astype(F32)
-            rows_bf[z, g, f] = res_ref[f, g].astype(BF16)
-
-            @pl.when(z < last)
-            def _():
-                row_copy(UP, z, f, g).start()
-
-            @pl.when(z > 0)
-            def _():
-                row_copy(DOWN, z, f, g).start()
-        loop(0, nf, finish)
-
-    arrivals = []
-    for i in range(GROUPS - 1):
-        options = ARRIVALS[i]
-        value = jnp.int32(options[0])
-        for at in range(1, GROUPS):
-            value = jnp.where(z == at, jnp.int32(options[at]), value)
-        arrivals.append(value)
-
-    for g in range(2):
-        give_back(z, g)
-    for r in arrivals:
-        for g in range(2):
-            def pass_on(f, r=r, g=g):
-                row_copy(UP, r, f, g).wait_recv()
-
-                @pl.when(jnp.logical_and(r < z, z < last))
-                def _():
-                    row_copy(UP, r, f, g).start()
-
-                @pl.when(jnp.logical_and(r > z, z > 0))
-                def _():
-                    row_copy(DOWN, r, f, g).start()
-            loop(0, nf, pass_on)
-            give_back(r, g)
+                for g in range(2):
+                    wait_plane(group(2), g)
+                    wait_plane(z, g)
+            for first, task in tasks:
+                @pl.when(jnp.logical_and(i >= first, i < first + pieces))
+                def _(first=first, task=task):
+                    p = i - first
+                    g = jnp.where(p >= nf, 1, 0)
+                    task(p - g * nf, g)
+            for at, c, g in handed:
+                @pl.when(i == at)
+                def _(c=c, g=g):
+                    give_back(group(c), g)
+        loop(0, 3 * pieces + 2 * LAG, step)
+        give_back(group(2), 1)
 
     for r in range(GROUPS):
         for g in range(2):
@@ -285,10 +313,6 @@
                 def _():
                     row_copy(DOWN, r, f, g).wait_send()
             loop(0, nf, hopped)
-
-
-ORDERS = ((3, 3, 0, 0), (2, 0, 3, 1), (1, 2, 1, 2), (0, 1, 2, 3))
-ARRIVALS = ((1, 0, 3, 2), (2, 2, 1, 1), (3, 3, 0, 0))
 
 
 def per_device(data, wavelet, panel_block, tiles, cover_rows, cover_freqs):

time: 98.7 us -> 90.9 us (0.921)
  Pallas kernels: 93.2 us -> 85.3 us
    pallas_call x1, Pallas kernels: 93.2 us -> 85.3 us  [per_device(): pl.pallas_call(functools.partial(kernel, n), out_shape=(jax.ShapeDtypeStr...]
where the time goes in v3:
time: 90.9 us; the launch traced here: 90.7 us
  Pallas kernels  85.3 us (94%)
  local copies, waits for them, and re-layouts  4.04 us (4%)
  between operations  1.31 us (1%)
    pallas_call x1, Pallas kernels, per_device(): pl.pallas_call(functools.partial(kernel, n), out_shape=(jax.ShapeDtypeStr...  85.3 us
    unnamed x7, local copies, waits for them, and re-layouts  4.04 us

profile of v3, /device:TPU:0, one launch (start us, length us, event | category | flops | bytes accessed | tf_op | source)
XLA Modules:
  0.0 90.7 jit_solution(10137283819429050333)
XLA Ops:
  0.6 0.0 copy-start.1
  1.3 0.0 copy-done.1
  1.3 0.7 copy.8.wav_ref
  2.0 85.3 %shard_map.77 = (f32[8,2,128,128]{3,2,1,0:T(8,128)}, bf16[16,2,128,128]{3,2,1,0:T(8,128)(2,1)}) custom-call(f32[8,2]{1,0:T(8,128)} %copy.8.wav_ref, s32[1]{0:T(128)S(6)} %copy.11.panel_ref, s32[16]{0:T(128)} %rows_ref.1, s32[16]{0:T(128)} %freqs_ref.1, bf16[8,2,128,128]{3,2,1,0:T(8,128)(2,1)} %data_ref.1, bf16[16,2,128,128]{3,2,1,0:T(8,128)(2,1)} %tiles_ref.1), custom_call_target="tpu_custom_call" | custom-call | tf_op jit(solution)/shard_map/pallas_call | solution.py:328
  87.3 0.0 copy-start
  87.3 2.4 %copy.12 = f32[8,2,128,128]{3,2,1,0:T(8,128)} copy(f32[8,2,128,128]{3,2,1,0:T(8,128)} %get-tuple-element.4) | data formatting | bytes 2097152
  89.7 0.0 copy-done
  89.7 1.0 %copy.13 = bf16[16,2,128,128]{3,2,1,0:T(8,128)(2,1)} copy(bf16[16,2,128,128]{3,2,1,0:T(8,128)(2,1)S(1)} %copy-done) | data formatting | bytes 2097152
Async XLA Ops:
  0.6 0.7 copy-start.1
  87.3 2.4 %copy-start = (bf16[16,2,128,128]{3,2,1,0:T(8,128)(2,1)S(1)}, bf16[16,2,128,128]{3,2,1,0:T(8,128)(2,1)}, u32[]{:S(2)}) copy-start(bf16[16,2,128,128]{3,2,1,0:T(8,128)(2,1)} %get-tuple-element.5) | copy-start | bytes 3145732

commit v4 on v3

--- a/solution.py
+++ b/solution.py
@@ -291,7 +291,10 @@
         out = (-out * scale).astype(BF16)
         grad_ref[t, 0] = out[:, :nb]
         grad_ref[t, 1] = out[:, nb:]
-    loop(0, slots, make_gradient)
+    def gradients(i, carry):
+        make_gradient(i)
+        return carry
+    lax.fori_loop(0, slots, gradients, 0, unroll=4)
 
     for r in range(GROUPS):
         for g in range(2):

time: 90.9 us -> 88.9 us (0.978)
  Pallas kernels: 85.3 us -> 83.3 us
    pallas_call x1, Pallas kernels: 85.3 us -> 83.3 us  [per_device(): pl.pallas_call(functools.partial(kernel, n), out_shape=(jax.ShapeDtypeStr...]
where the time goes in v4:
time: 88.9 us; the launch traced here: 88.7 us
  Pallas kernels  83.3 us (94%)
  local copies, waits for them, and re-layouts  4.04 us (5%)
  between operations  1.31 us (1%)
    pallas_call x1, Pallas kernels, per_device(): pl.pallas_call(functools.partial(kernel, n), out_shape=(jax.ShapeDtypeStr...  83.3 us
    unnamed x7, local copies, waits for them, and re-layouts  4.04 us

profile of v4, /device:TPU:0, one launch (start us, length us, event | category | flops | bytes accessed | tf_op | source)
XLA Modules:
  0.0 88.7 jit_solution(4514759727125992830)
XLA Ops:
  0.6 0.0 copy-start.1
  1.3 0.0 copy-done.1
  1.3 0.7 copy.8.wav_ref
  2.0 83.3 %shard_map.77 = (f32[8,2,128,128]{3,2,1,0:T(8,128)}, bf16[16,2,128,128]{3,2,1,0:T(8,128)(2,1)}) custom-call(f32[8,2]{1,0:T(8,128)} %copy.8.wav_ref, s32[1]{0:T(128)S(6)} %copy.11.panel_ref, s32[16]{0:T(128)} %rows_ref.1, s32[16]{0:T(128)} %freqs_ref.1, bf16[8,2,128,128]{3,2,1,0:T(8,128)(2,1)} %data_ref.1, bf16[16,2,128,128]{3,2,1,0:T(8,128)(2,1)} %tiles_ref.1), custom_call_target="tpu_custom_call" | custom-call | tf_op jit(solution)/shard_map/pallas_call | solution.py:331
  85.3 0.0 copy-start
  85.3 2.4 %copy.12 = f32[8,2,128,128]{3,2,1,0:T(8,128)} copy(f32[8,2,128,128]{3,2,1,0:T(8,128)} %get-tuple-element.4) | data formatting | bytes 2097152
  87.7 0.0 copy-done
  87.7 1.0 %copy.13 = bf16[16,2,128,128]{3,2,1,0:T(8,128)(2,1)} copy(bf16[16,2,128,128]{3,2,1,0:T(8,128)(2,1)S(1)} %copy-done) | data formatting | bytes 2097152
Async XLA Ops:
  0.6 0.7 copy-start.1
  85.3 2.4 %copy-start = (bf16[16,2,128,128]{3,2,1,0:T(8,128)(2,1)S(1)}, bf16[16,2,128,128]{3,2,1,0:T(8,128)(2,1)}, u32[]{:S(2)}) copy-start(bf16[16,2,128,128]{3,2,1,0:T(8,128)(2,1)} %get-tuple-element.5) | copy-start | bytes 3145732
